TPU v7x, 32 devices: a whole 2x2x4 slice. The times are simulated.
32 devices in a mesh: grp: 2 (over y), cell: 16 (over z, x, core).
Axes of the slice: x: 2, y: 2, z: 4, core: 2. Of those that a mesh axis runs over, the one named last changes fastest.
Arguments:
- momenta: int32 [3, 65536], replicated, may hold values from 1 to 32
- positions: float32 [3, 4096], P(None, ('grp', 'cell')), parts along dimension 1, may hold values from 0 to 1
- weights: bfloat16 [8, 4096], P(None, ('grp', 'cell')), parts along dimension 1, may hold values from 0.099609375 to 2
- triplets: int32 [3, 16384], P(None, ('grp', 'cell')), parts along dimension 1, may hold values from 0 to 65535, as said below
- cotangent: float32 [8, 16384], P(None, ('grp', 'cell')), parts along dimension 1, may hold values from -6 to 6
Outputs:
- correlation: float32 [8, 16384], P(None, ('grp', 'cell')), parts along dimension 1
- weight_grad: float32 [8, 4096], P(None, ('grp', 'cell')), parts along dimension 1
There are 2 independent parts, one for each index of `grp`. A program takes and returns all parts, laid end to end along the dimension named above; an argument that names none is the same for every part. Nothing has to cross between parts.
Inputs may be any that keep to these rules, and one draw needn't show every extreme that they name: Among the 1536 momentum indices of one device's triplets, each block of 4096 momenta (4096 * r to 4096 * r + 4095) is named either 96 - 1 or 96 times.
All inputs are finite; a program needn't handle non-finite values.
Results may differ from a plain program's by a relative error of at most 0.0051.
Values may be sent and summed in bfloat16 or wider, within the bound.
No kernel may reach another device: no remote copies, remote signals or barrier semaphores. Data moves between devices by JAX's collectives and lax.ppermute only.
A program may use at most 256 MiB of HBM per device.

v0:
```python
import math
import jax
import jax.numpy as jnp
from jax import lax
from jax.sharding import PartitionSpec as P

TWO_PI = 2.0 * math.pi


def tables(moment_block, position_block):
    numbers = moment_block.astype(jnp.float32)
    phase = numbers[0][:, None] * position_block[0][None, :]
    phase = phase + numbers[1][:, None] * position_block[1][None, :]
    phase = phase + numbers[2][:, None] * position_block[2][None, :]
    phase = TWO_PI * phase
    return (jnp.cos(phase).astype(jnp.bfloat16), jnp.sin(phase).astype(jnp.bfloat16))


def contract(left, right):
    return lax.dot_general(
        left, right, (((1,), (1,)), ((), ())), preferred_element_type=jnp.float32
    )


def amplitude_term(moment_block, position_block, weight_block):
    cosine, sine = tables(moment_block, position_block)
    return jnp.concatenate([contract(weight_block, cosine), contract(weight_block, sine)], 0)


def gradient_term(adjoint_block, moment_block, position_block):
    cosine, sine = tables(moment_block, position_block)
    bin_count = adjoint_block.shape[0] // 2
    return jnp.dot(adjoint_block[:bin_count], cosine, preferred_element_type=jnp.float32) + jnp.dot(
        adjoint_block[bin_count:], sine, preferred_element_type=jnp.float32
    )


def couple(cotangent, real_one, imag_one, real_two, imag_two):
    real_part = cotangent * (real_one * real_two - imag_one * imag_two)
    imag_part = -cotangent * (imag_one * real_two + real_one * imag_two)
    return jnp.concatenate([real_part, imag_part], 0)


def triplet_terms(amplitude, triplets, cotangent, bin_count):
    real_rows = amplitude[:bin_count]
    imag_rows = amplitude[bin_count:]
    real_a = real_rows[:, triplets[0]]
    real_b = real_rows[:, triplets[1]]
    real_c = real_rows[:, triplets[2]]
    imag_a = imag_rows[:, triplets[0]]
    imag_b = imag_rows[:, triplets[1]]
    imag_c = imag_rows[:, triplets[2]]
    correlation = (
        real_a * real_b * real_c
        - real_a * imag_b * imag_c
        - imag_a * real_b * imag_c
        - imag_a * imag_b * real_c
    )
    adjoint = jnp.zeros(amplitude.shape, jnp.float32)
    adjoint = adjoint.at[:, triplets[0]].add(couple(cotangent, real_b, imag_b, real_c, imag_c))
    adjoint = adjoint.at[:, triplets[1]].add(couple(cotangent, real_a, imag_a, real_c, imag_c))
    adjoint = adjoint.at[:, triplets[2]].add(couple(cotangent, real_a, imag_a, real_b, imag_b))
    return (correlation, adjoint)


def spread(owned_part):
    return lax.all_gather(owned_part, "cell", axis=1, tiled=True)


def on_device(momenta, positions, weights, triplets, cotangent):
    devices = lax.axis_size("cell")
    bin_count = weights.shape[0]
    moment_count = momenta.shape[1]
    local_cells = positions.shape[1]
    all_cells = local_cells * devices
    norm_factor = 1.0 / math.sqrt(all_cells)
    moment_step = min(moment_count, 4096)
    moment_blocks = moment_count // moment_step
    full_amp = None

    def forward_cells(index, buffer):
        start = index * moment_step
        moment_block = lax.dynamic_slice_in_dim(momenta, start, moment_step, 1)
        term = amplitude_term(moment_block, positions, weights)
        return lax.dynamic_update_slice_in_dim(buffer, term, start, 1)

    partial_sums = lax.fori_loop(
        0, moment_blocks, forward_cells, jnp.zeros((2 * bin_count, moment_count), jnp.float32)
    )
    owned_amp = (
        lax.psum_scatter(partial_sums, "cell", scatter_dimension=1, tiled=True) * norm_factor
    )
    amplitude = spread(owned_amp)
    correlation, adjoint = triplet_terms(amplitude, triplets, cotangent, bin_count)
    owned_sum = lax.psum_scatter(adjoint, "cell", scatter_dimension=1, tiled=True)
    owned_adjoint = (owned_sum * norm_factor).astype(jnp.bfloat16)
    full_adjoint = lax.all_gather(owned_adjoint, "cell", axis=1, tiled=True)

    def backward_cells(index, summed):
        start = index * moment_step
        moment_block = lax.dynamic_slice_in_dim(momenta, start, moment_step, 1)
        adjoint_block = lax.dynamic_slice_in_dim(full_adjoint, start, moment_step, 1)
        return summed + gradient_term(adjoint_block, moment_block, positions)

    weight_grad = lax.fori_loop(
        0, moment_blocks, backward_cells, jnp.zeros((bin_count, local_cells), jnp.float32)
    )
    return (correlation, weight_grad)


def solution(mesh):
    placed = (
        P(),
        P(None, ("grp", "cell")),
        P(None, ("grp", "cell")),
        P(None, ("grp", "cell")),
        P(None, ("grp", "cell")),
    )
    return jax.shard_map(
        on_device,
        mesh=mesh,
        in_specs=placed,
        out_specs=(P(None, ("grp", "cell")), P(None, ("grp", "cell"))),
        check_vma=False,
    )
```

profile of v0, /device:TPU:0, one launch (start us, length us, event | category | flops | bytes accessed | tf_op | source)
XLA Modules:
  0.0 1721.1 jit_solution(12182722601391225925)
XLA Ops:
  9.6 271.4 %while.27 = (s32[]{:T(128)}, f32[16,65536]{1,0:T(8,128)}, s32[3,65536]{1,0:T(4,128)}, f32[3,128]{1,0:T(4,128)S(1)}, bf16[8,128]{1,0:T(8,128)(2,1)S(1)}, /*index=5*/s32[]{:T(128)}, s32[]{:T(128)}, s32[]{:T(128)}, s32[]{:T(128)}) while((s32[]{:T(128)}, f32[16,65536]{1,0:T(8,128)}, s32[3,65536]{1,0:T(4,128)}, f32[3,128]{1,0:T(4,128)S(1)}, ...), condition=%wide.region_1.0_spmd, body=%wide.region_0.0_spmd.sunk | while | flops 24195076 | bytes 1091739 | solution.py:87
  10.5 7.7 convolution_bitcast_fusion.4
  27.4 7.7 convolution_bitcast_fusion.4
  44.4 7.7 convolution_bitcast_fusion.4
  61.4 7.7 convolution_bitcast_fusion.4
  78.3 7.7 convolution_bitcast_fusion.4
  95.3 7.7 convolution_bitcast_fusion.4
  112.3 7.7 convolution_bitcast_fusion.4
  129.2 7.7 convolution_bitcast_fusion.4
  146.1 7.7 convolution_bitcast_fusion.4
  163.1 7.7 convolution_bitcast_fusion.4
  180.0 7.7 convolution_bitcast_fusion.4
  197.0 7.7 convolution_bitcast_fusion.4
  214.0 7.7 convolution_bitcast_fusion.4
  264.8 7.7 convolution_bitcast_fusion.4
  281.0 16.9 copy.53
  298.0 333.3 %reduce-scatter.3.cloned.1.call-done = f32[16,4096]{0,1:T(8,128)} async-done(((f32[16,65536]{0,1:T(8,128)}), f32[16,4096]{0,1:T(8,128)}) %reduce-scatter.3.cloned.1.call-update) | async-done | bytes 262160 | tf_op jit(solution)/shard_map/reduce_scatter | solution.py:91
  635.2 166.6 %all-gather.3.cloned.1.call-done = f32[16,65536]{0,1:T(8,128)} async-done(((f32[16,4096]{0,1:T(8,128)}), f32[16,65536]{0,1:T(8,128)}) %all-gather.3.cloned.1.call-update) | async-done | bytes 4194320 | tf_op jit(solution)/shard_map/all_gather | solution.py:67
  801.8 44.5 %fusion.44 = (f32[8,65536]{0,1:T(8,128)}, f32[8,65536]{0,1:T(8,128)}) fusion(f32[16,65536]{0,1:T(8,128)} %all-gather.3.cloned.1.call-done), kind=kLoop, calls=%fused_computation.100 | loop fusion | bytes 8388608 | tf_op jit(solution)/shard_map/slice | solution.py:45
  846.3 11.6 gather_fusion.1
  857.9 11.6 gather_fusion
  869.5 11.6 gather_fusion.3
  881.0 11.6 gather_fusion.5
  892.6 11.6 gather_fusion.4
  904.2 11.6 gather_fusion.2
  917.2 15.4 scatter_custom_fusion
  932.9 24.6 %scatter_fusion = f32[16,65536]{0,1:T(8,128)} fusion(f32[16,65536]{0,1:T(8,128)} %scatter_custom_fusion, s32[512]{0:T(512)S(1)} %bitcast.180, f32[512,16]{1,0:T(8,128)S(1)} %copy.61), kind=kCustom, calls=%fused_computation.7 | custom fusion | flops 8192 | bytes 100352 | tf_op jit(solution)/shard_map/scatter-add | solution.py:61
  957.5 24.6 %scatter_fusion.1 = f32[16,65536]{0,1:T(8,128)} fusion(f32[16,65536]{0,1:T(8,128)} %scatter_fusion, s32[512]{0:T(512)S(1)} %bitcast.178, f32[512,16]{1,0:T(8,128)S(1)} %copy.62), kind=kCustom, calls=%fused_computation.8 | custom fusion | flops 8192 | bytes 100352 | tf_op jit(solution)/shard_map/scatter-add | solution.py:62
  982.1 330.6 %reduce-scatter.5.cloned.1.call-done = f32[16,4096]{0,1:T(8,128)} async-done(((f32[16,65536]{0,1:T(8,128)}), f32[16,4096]{0,1:T(8,128)}) %reduce-scatter.5.cloned.1.call-update) | async-done | bytes 262160 | tf_op jit(solution)/shard_map/reduce_scatter | solution.py:95
  1315.5 125.7 %all-gather.5.cloned.1.call-done = bf16[16,65536]{0,1:T(8,128)(2,1)} async-done(((bf16[16,4096]{0,1:T(8,128)(2,1)}), bf16[16,65536]{0,1:T(8,128)(2,1)}) %all-gather.5.cloned.1.call-update) | async-done | bytes 2097168 | tf_op jit(solution)/shard_map/all_gather | solution.py:97
  1441.2 12.8 copy.63
  1454.0 259.5 %while.28 = (s32[]{:T(128)}, f32[8,128]{1,0:T(8,128)S(1)}, bf16[16,65536]{1,0:T(8,128)(2,1)S(1)}, s32[3,65536]{1,0:T(4,128)}, f32[3,128]{1,0:T(4,128)S(1)}, /*in...) while((s32[]{:T(128)}, f32[8,128]{1,0:T(8,128)S(1)}, bf16[16,65536]{1,0:T(8,128)(2,1)S(1)}, ...), condition=%wide.region_8.0_spmd.clone, body=%wide.region_7.0_spmd.clone.sunk | while | flops 24132616 | bytes 448705 | solution.py:105
  (200 shorter events, 433.9 us)
Async XLA Ops:
  7.2 624.1 %reduce-scatter.3.cloned.1.call-start = ((), (), s32[]{:S(2)}) async-start(), calls=%async_computation.2 | async-start | bytes 35651584 | tf_op jit(solution)/shard_map/reduce_scatter | solution.py:91
  7.2 2.4 copy-start
  7.2 2.4 copy-start.3
  297.9 503.9 %all-gather.3.cloned.1.call-start = ((), (), s32[]{:S(2)}) async-start(), calls=%async_computation.3 | async-start | bytes 35651584 | tf_op jit(solution)/shard_map/all_gather | solution.py:67
  634.5 0.7 copy-start.2
  634.5 678.3 %reduce-scatter.5.cloned.1.call-start = ((), (), s32[]{:S(2)}) async-start(), calls=%async_computation.4 | async-start | bytes 35651584 | tf_op jit(solution)/shard_map/reduce_scatter | solution.py:95
  846.3 70.1 %copy-start.1 = (f32[8,512]{1,0:T(8,128)S(1)}, f32[8,512]{1,0:T(8,128)}, u32[]{:S(2)}) copy-start(f32[8,512]{1,0:T(8,128)} %param.13) | copy-start | bytes 49156
  982.1 459.1 %all-gather.5.cloned.1.call-start = ((), (), s32[]{:S(2)}) async-start(), calls=%async_computation.5 | async-start | bytes 17825792 | tf_op jit(solution)/shard_map/all_gather | solution.py:97
  1713.6 0.6 copy-start.4
Sparse Core Ops, SparseCore 0:
  298.0 333.2 reduce-scatter.2
  634.6 167.1 all-gather.2
  982.2 330.5 reduce-scatter.4
  1315.7 125.5 all-gather.4
where the time goes:
time: 1730 us; the launch traced here: 1720 us
  waiting for transfers between devices  956 us (55%)
  matrix products  490 us (28%)
  local copies, waits for them, and re-layouts  149 us (9%)
  other arithmetic  110 us (6%)
    reduce_scatter x1, waiting for transfers between devices, on_device(): lax.psum_scatter(partial_sums, 'cell', scatter_dimension=1, tiled=True)  333 us
    reduce_scatter x1, waiting for transfers between devices, on_device(): lax.psum_scatter(adjoint, 'cell', scatter_dimension=1, tiled=True)  331 us
    dot_general x32, matrix products, contract(): lax.dot_general(left, right, (((1,), (1,)), ((), ())), preferred_element_...  245 us
    all_gather x1, waiting for transfers between devices, spread(): return lax.all_gather(owned_part, 'cell', axis=1, tiled=True)  167 us
    all_gather x1, waiting for transfers between devices, on_device(): full_adjoint = lax.all_gather(owned_adjoint, 'cell', axis=1, tiled=True)  126 us
    dot_general x16, matrix products, gradient_term(): jnp.dot(adjoint_block[bin_count:], sine, preferred_element_type=jnp.float32)  123 us
    dot_general x16, matrix products, gradient_term(): jnp.dot(adjoint_block[:bin_count], cosine, preferred_element_type=jnp.flo...  122 us
    slice x1, local copies, waits for them, and re-layouts, triplet_terms(): real_rows = amplitude[:bin_count]  44.5 us
  transfers between devices with their start and end apart: 4, of which 4 were waited for; matrix products, arithmetic and copies ran while one was open for 0% of the time, Pallas kernels for 0%

commit v1 on v0

--- a/solution.py
+++ b/solution.py
@@ -5,6 +5,18 @@
 from jax.sharding import PartitionSpec as P
 
 TWO_PI = 2.0 * math.pi
+
+
+def doubled_up(x, axis, dim):
+    ways, here = (lax.axis_size(axis), lax.axis_index(axis))
+    grown, reach = (x, 1)
+    while reach < ways:
+        theirs = lax.ppermute(grown, axis, [(d, d ^ reach) for d in range(ways)])
+        mine_first = jnp.concatenate([grown, theirs], axis=dim)
+        theirs_first = jnp.concatenate([theirs, grown], axis=dim)
+        grown = jnp.where(here & reach == 0, mine_first, theirs_first)
+        reach = 2 * reach
+    return grown
 
 
 def tables(moment_block, position_block):
@@ -94,7 +106,7 @@
     correlation, adjoint = triplet_terms(amplitude, triplets, cotangent, bin_count)
     owned_sum = lax.psum_scatter(adjoint, "cell", scatter_dimension=1, tiled=True)
     owned_adjoint = (owned_sum * norm_factor).astype(jnp.bfloat16)
-    full_adjoint = lax.all_gather(owned_adjoint, "cell", axis=1, tiled=True)
+    full_adjoint = doubled_up(owned_adjoint, "cell", 1)
 
     def backward_cells(index, summed):
         start = index * moment_step

time: 1730 us -> 1030 us (0.60)
  waiting for transfers between devices: 956 us -> 264 us
  local copies, waits for them, and re-layouts: 149 us -> 130 us
    reduce_scatter x1, waiting for transfers between devices: 331 us -> 71.4 us  [on_device(): lax.psum_scatter(adjoint, 'cell', scatter_dimension=1, tiled=True)]
    reduce_scatter x1, waiting for transfers between devices: 333 us -> 75.6 us  [on_device(): lax.psum_scatter(partial_sums, 'cell', scatter_dimension=1, tiled=True)]
    all_gather x1 -> x0, waiting for transfers between devices: 126 us -> none  [on_device(): full_adjoint = lax.all_gather(owned_adjoint, 'cell', axis=1, tiled=True)]
    all_gather x1, waiting for transfers between devices: 167 us -> 49.8 us  [spread(): return lax.all_gather(owned_part, 'cell', axis=1, tiled=True)]
    ppermute x0 -> x4, waiting for transfers between devices: none -> 67.2 us  [doubled_up(): theirs = lax.ppermute(grown, axis, [(d, d ^ reach) for d in range(ways)])]
    slice x1 -> x2, local copies, waits for them, and re-layouts: 44.5 us -> 20.1 us  [triplet_terms(): real_rows = amplitude[:bin_count]]
    scatter-add x0 -> x1, local copies, waits for them, and re-layouts: none -> 19.1 us  [triplet_terms(): adjoint.at[:, triplets[2]]]
  transfers between devices with their start and end apart: 4 -> 7, of which waited for: 4 -> 7; matrix products, arithmetic and copies ran while one was open for 0% -> 0% of each run, Pallas kernels for 0% -> 0%
where the time goes in v1:
time: 1030 us; the launch traced here: 1010 us
  matrix products  490 us (48%)
  waiting for transfers between devices  264 us (26%)
  local copies, waits for them, and re-layouts  130 us (13%)
  other arithmetic  109 us (11%)
  between operations  14.3 us (1%)
    dot_general x32, matrix products, contract(): lax.dot_general(left, right, (((1,), (1,)), ((), ())), preferred_element_...  245 us
    dot_general x16, matrix products, gradient_term(): jnp.dot(adjoint_block[bin_count:], sine, preferred_element_type=jnp.float32)  123 us
    dot_general x16, matrix products, gradient_term(): jnp.dot(adjoint_block[:bin_count], cosine, preferred_element_type=jnp.flo...  122 us
    reduce_scatter x1, waiting for transfers between devices, on_device(): lax.psum_scatter(partial_sums, 'cell', scatter_dimension=1, tiled=True)  75.6 us
    reduce_scatter x1, waiting for transfers between devices, on_device(): lax.psum_scatter(adjoint, 'cell', scatter_dimension=1, tiled=True)  71.4 us
    ppermute x4, waiting for transfers between devices, doubled_up(): theirs = lax.ppermute(grown, axis, [(d, d ^ reach) for d in range(ways)])  67.2 us
    all_gather x1, waiting for transfers between devices, spread(): return lax.all_gather(owned_part, 'cell', axis=1, tiled=True)  49.8 us
    convert_element_type x32, other arithmetic, tables(): numbers = moment_block.astype(jnp.float32)  27.3 us
  transfers between devices with their start and end apart: 7, of which 7 were waited for; matrix products, arithmetic and copies ran while one was open for 0% of the time, Pallas kernels for 0%

profile of v1, /device:TPU:0, one launch (start us, length us, event | category | flops | bytes accessed | tf_op | source)
XLA Modules:
  0.0 1011.6 jit_solution(5152646143350467079)
XLA Ops:
  9.5 271.3 %while.27 = (s32[]{:T(128)}, f32[16,65536]{1,0:T(8,128)}, s32[3,65536]{1,0:T(4,128)}, f32[3,128]{1,0:T(4,128)S(1)}, bf16[8,128]{1,0:T(8,128)(2,1)S(1)}, /*index=5*/s32[]{:T(128)}, s32[]{:T(128)}, s32[]{:T(128)}, s32[]{:T(128)}) while((s32[]{:T(128)}, f32[16,65536]{1,0:T(8,128)}, s32[3,65536]{1,0:T(4,128)}, f32[3,128]{1,0:T(4,128)S(1)}, ...), condition=%wide.region_1.0_spmd, body=%wide.region_0.0_spmd.sunk | while | flops 24195076 | bytes 1091731 | solution.py:99
  18.0 7.7 convolution_bitcast_fusion.4
  34.9 7.7 convolution_bitcast_fusion.4
  51.9 7.7 convolution_bitcast_fusion.4
  85.8 7.7 convolution_bitcast_fusion.4
  102.7 7.7 convolution_bitcast_fusion.4
  119.6 7.7 convolution_bitcast_fusion.4
  136.6 7.7 convolution_bitcast_fusion.4
  170.5 7.7 convolution_bitcast_fusion.4
  204.4 7.7 convolution_bitcast_fusion.4
  221.3 7.7 convolution_bitcast_fusion.4
  238.3 7.7 convolution_bitcast_fusion.4
  255.3 7.7 convolution_bitcast_fusion.4
  280.9 75.6 %reduce-scatter.3.cloned.1.call-done = f32[16,4096]{1,0:T(8,128)} async-done(((f32[16,65536]{1,0:T(8,128)}), f32[16,4096]{1,0:T(8,128)}) %reduce-scatter.3.cloned.1.call-update) | async-done | bytes 262160 | tf_op jit(solution)/shard_map/reduce_scatter | solution.py:103
  358.3 49.8 %all-gather.2.cloned.1.call-done = f32[16,65536]{1,0:T(8,128)} async-done(((f32[16,4096]{1,0:T(8,128)}), f32[16,65536]{1,0:T(8,128)}) %all-gather.2.cloned.1.call-update) | async-done | bytes 4194320 | tf_op jit(solution)/shard_map/all_gather | solution.py:79
  411.9 16.3 %copy.55 = f32[8,65536]{0,1:T(8,128)} copy(f32[8,65536]{1,0:T(8,128)} %get-tuple-element.278) | data formatting | bytes 4194304 | tf_op jit(solution)/shard_map/slice | solution.py:57
  428.2 11.6 %gather_fusion.1 = f32[512,8]{1,0:T(8,128)S(1)} fusion(f32[8,65536]{0,1:T(8,128)} %copy.55, s32[1024]{0:T(1024)S(1)} %pad_clamp_fusion.1), kind=kCustom, calls=%fused_computation.1 | custom fusion | bytes 34816 | tf_op jit(solution)/shard_map/gather | solution.py:60
  439.8 11.6 %gather_fusion.2 = f32[512,8]{1,0:T(8,128)S(1)} fusion(f32[8,65536]{0,1:T(8,128)} %copy.55, s32[1024]{0:T(1024)S(1)} %pad_clamp_fusion), kind=kCustom, calls=%fused_computation.2 | custom fusion | bytes 34816 | tf_op jit(solution)/shard_map/gather | solution.py:61
  451.4 16.5 %copy.61 = f32[8,65536]{0,1:T(8,128)} copy(f32[8,65536]{1,0:T(8,128)S(1)} %get-tuple-element.279) | data formatting | bytes 4194304 | tf_op jit(solution)/shard_map/slice | solution.py:58
  467.9 11.6 %gather_fusion.3 = f32[512,8]{1,0:T(8,128)S(1)} fusion(f32[8,65536]{0,1:T(8,128)} %copy.61, s32[1024]{0:T(1024)S(1)} %pad_clamp_fusion.1), kind=kCustom, calls=%fused_computation.3 | custom fusion | bytes 34816 | tf_op jit(solution)/shard_map/gather | solution.py:63
  479.5 11.6 %gather_fusion.4 = f32[512,8]{1,0:T(8,128)S(1)} fusion(f32[8,65536]{0,1:T(8,128)} %copy.61, s32[1024]{0:T(1024)S(1)} %pad_clamp_fusion), kind=kCustom, calls=%fused_computation.4 | custom fusion | bytes 34816 | tf_op jit(solution)/shard_map/gather | solution.py:64
  491.1 11.6 %gather_fusion = f32[512,8]{1,0:T(8,128)S(1)} fusion(f32[8,65536]{0,1:T(8,128)} %copy.55, s32[1024]{0:T(1024)S(1)} %pad_clamp_fusion.2), kind=kCustom, calls=%fused_computation | custom fusion | bytes 34816 | tf_op jit(solution)/shard_map/gather | solution.py:59
  502.7 11.6 %gather_fusion.5 = f32[512,8]{1,0:T(8,128)S(1)} fusion(f32[8,65536]{0,1:T(8,128)} %copy.61, s32[1024]{0:T(1024)S(1)} %pad_clamp_fusion.2), kind=kCustom, calls=%fused_computation.5 | custom fusion | bytes 34816 | tf_op jit(solution)/shard_map/gather | solution.py:62
  515.6 15.4 %scatter_custom_fusion = f32[16,65536]{0,1:T(8,128)} fusion(s32[512]{0:T(512)S(1)} %bitcast.182, f32[512,16]{1,0:T(8,128)S(1)} %copy.67, f32[]{:T(128)} %constant.82.clone.1), kind=kCustom, calls=%fused_computation.56 | custom fusion | flops 8192 | bytes 4194308 | tf_op jit(solution)/shard_map/scatter-add | solution.py:72
  531.3 24.6 %scatter_fusion = f32[16,65536]{0,1:T(8,128)} fusion(f32[16,65536]{0,1:T(8,128)} %scatter_custom_fusion, s32[512]{0:T(512)S(1)} %bitcast.180, f32[512,16]{1,0:T(8,128)S(1)} %copy.68), kind=kCustom, calls=%fused_computation.7 | custom fusion | flops 8192 | bytes 100352 | tf_op jit(solution)/shard_map/scatter-add | solution.py:73
  555.9 24.6 %scatter_fusion.1 = f32[16,65536]{0,1:T(8,128)} fusion(f32[16,65536]{0,1:T(8,128)} %scatter_fusion, s32[512]{0:T(512)S(1)} %bitcast.178, f32[512,16]{1,0:T(8,128)S(1)} %copy.69), kind=kCustom, calls=%fused_computation.8 | custom fusion | flops 8192 | bytes 100352 | tf_op jit(solution)/shard_map/scatter-add | solution.py:74
  580.5 19.1 %copy.70 = f32[16,65536]{1,0:T(8,128)} copy(f32[16,65536]{0,1:T(8,128)} %scatter_fusion.1) | data formatting | bytes 8388608 | tf_op jit(solution)/shard_map/scatter-add | solution.py:74
  599.6 71.4 %reduce-scatter.5.cloned.1.call-done = f32[16,4096]{1,0:T(8,128)} async-done(((f32[16,65536]{1,0:T(8,128)}), f32[16,4096]{1,0:T(8,128)}) %reduce-scatter.5.cloned.1.call-update) | async-done | bytes 262160 | tf_op jit(solution)/shard_map/reduce_scatter | solution.py:107
  674.1 7.9 collective-permute-done.1
  683.0 12.3 %collective-permute-done.2 = bf16[16,16384]{1,0:T(8,128)(2,1)S(1)} collective-permute-done((bf16[16,16384]{1,0:T(8,128)(2,1)S(1)}, bf16[16,16384]{1,0:T(8,128)(2,1)S(1)}, u32[]{:S(2)}, u32[]{:S(2)}) %collective-permute-start.2) | collective-permute-done | bytes 524320 | tf_op jit(solution)/shard_map/ppermute | solution.py:14
  696.9 45.7 %collective-permute-done.3 = bf16[16,32768]{1,0:T(8,128)(2,1)} collective-permute-done((bf16[16,32768]{1,0:T(8,128)(2,1)S(1)}, bf16[16,32768]{1,0:T(8,128)(2,1)}, u32[]{:S(2)}, u32[]{:S(2)}) %collective-permute-start.3) | collective-permute-done | bytes 1048608 | tf_op jit(solution)/shard_map/ppermute | solution.py:14
  744.6 259.6 %while.28 = (s32[]{:T(128)}, f32[8,128]{1,0:T(8,128)S(1)}, bf16[16,65536]{1,0:T(8,128)(2,1)S(1)}, s32[3,65536]{1,0:T(4,128)}, f32[3,128]{1,0:T(4,128)S(1)}, /*in...) while((s32[]{:T(128)}, f32[8,128]{1,0:T(8,128)S(1)}, bf16[16,65536]{1,0:T(8,128)(2,1)S(1)}, ...), condition=%wide.region_8.9_spmd.clone, body=%wide.region_7.8_spmd.clone.sunk | while | flops 24132616 | bytes 448697 | solution.py:117
  (210 shorter events, 455.3 us)
Async XLA Ops:
  7.2 349.3 %reduce-scatter.3.cloned.1.call-start = ((), (), s32[]{:S(2)}) async-start(), calls=%async_computation.2 | async-start | bytes 4456448 | tf_op jit(solution)/shard_map/reduce_scatter | solution.py:103
  7.2 2.2 copy-start
  7.2 2.2 copy-start.3
  280.8 77.4 %copy-start.2 = (s32[3,512]{1,0:T(4,128)S(1)}, s32[3,512]{1,0:T(4,128)}, u32[]{:S(2)}) copy-start(s32[3,512]{1,0:T(4,128)} %param.12) | copy-start | bytes 18436
  280.8 127.3 %all-gather.2.cloned.1.call-start = ((), (), s32[]{:S(2)}) async-start(), calls=%async_computation.3 | async-start | bytes 4456448 | tf_op jit(solution)/shard_map/all_gather | solution.py:79
  358.2 312.9 %reduce-scatter.5.cloned.1.call-start = ((), (), s32[]{:S(2)}) async-start(), calls=%async_computation.4 | async-start | bytes 4456448 | tf_op jit(solution)/shard_map/reduce_scatter | solution.py:107
  467.9 47.0 %copy-start.1 = (f32[8,512]{1,0:T(8,128)S(1)}, f32[8,512]{1,0:T(8,128)}, u32[]{:S(2)}) copy-start(f32[8,512]{1,0:T(8,128)} %param.13) | copy-start | bytes 49156
  672.0 1.4 collective-permute-start
  673.5 8.4 collective-permute-start.1
  682.1 13.2 %collective-permute-start.2 = (bf16[16,16384]{1,0:T(8,128)(2,1)S(1)}, bf16[16,16384]{1,0:T(8,128)(2,1)S(1)}, u32[]{:S(2)}, u32[]{:S(2)}) collective-permute-start(bf16[16,16384]{1,0:T(8,128)(2,1)S(1)} %maximum_select_fusion.2), channel_id=1, source_target_pairs={{0,4},{1,5},{2,6},{3,7},{4,0},{5,1},{6,2},{7,3},{8,12},{9,13},{10,... | collective-permute-start | bytes 1572872 | tf_op jit(solution)/shard_map/ppermute | solution.py:14
  695.5 47.0 %collective-permute-start.3 = (bf16[16,32768]{1,0:T(8,128)(2,1)S(1)}, bf16[16,32768]{1,0:T(8,128)(2,1)}, u32[]{:S(2)}, u32[]{:S(2)}) collective-permute-start(bf16[16,32768]{1,0:T(8,128)(2,1)S(1)} %maximum_select_fusion.1), channel_id=1, source_target_pairs={{0,8},{1,9},{2,10},{3,11},{4,12},{5,13},{6,14},{7,15},{8,0},{9,1},... | collective-permute-start | bytes 3145736 | tf_op jit(solution)/shard_map/ppermute | solution.py:14
  1004.1 0.6 copy-start.4
Sparse Core Ops, SparseCore 0:
  280.9 75.4 reduce-scatter.2
  358.6 49.4 all-gather.1
  599.7 71.2 reduce-scatter.4
